TPU v7x, 32 devices: a whole 2x2x4 slice. The times are simulated.
32 devices in a mesh: tm: 8 (over z, y), scene: 4 (over x, core).
Axes of the slice: x: 2, y: 2, z: 4, core: 2. Of those that a mesh axis runs over, the one named last changes fastest.
Arguments:
- frames: bfloat16 [512, 2, 32, 384], P('tm', None, 'scene'), may hold values from -6 to 6
- conv_weight: bfloat16 [3, 3, 3, 384, 384], replicated, may hold values from -0.0625 to 0.0625
- down_weight: bfloat16 [8, 384, 384], replicated, may hold values from -0.109375 to 0.109375
- w_query: bfloat16 [384, 384], replicated, may hold values from -64 to 64
- w_key: bfloat16 [384, 384], replicated, may hold values from -2 to 2
- w_value: bfloat16 [384, 384], replicated, may hold values from -0.3125 to 0.3125
- w_out: bfloat16 [384, 384], replicated, may hold values from -0.3125 to 0.3125
- shot_lengths: int32 [4], replicated, may hold values from 1 to 32, 64 in all
- scene_label: int32 [64, 1], P('tm'), may hold values from 0 to 3; in each aligned block of 8 rows (0 to 7, 8 to 15, ...) at most 4 rows name the same one
- out_grad: bfloat16 [512, 2, 32, 384], P('tm', None, 'scene'), may hold values from -6 to 6
Outputs:
- latent_out: bfloat16 [64, 2, 32, 384], P('tm', None, 'scene')
- frame_grad: bfloat16 [512, 2, 32, 384], P('tm', None, 'scene')
Inputs may be any that keep to these rules, and one draw needn't show every extreme that they name: `shot_lengths`: the lengths sum to 64; the longest is exactly 32. `scene_label`: within each aligned block of 8 latent frames (those of one index of tm) no label occurs more than 4 times; in some block one label occurs exactly 4 times.
All inputs are finite; a program needn't handle non-finite values.
Results may differ from a plain program's by a relative error of at most 0.008.
Values may be sent and summed in bfloat16 or wider, within the bound.
A program may use at most 128 MiB of HBM per device.

v0:
```python
import functools
import math

import jax
import jax.numpy as jnp
from jax import lax
from jax.experimental import pallas as pl
from jax.experimental.pallas import tpu as pltpu
from jax.sharding import PartitionSpec as P

HEAD = 64
KT, KH, KW = 3, 3, 3
DOWN = 8
LANES = 128
VMEM_MIB = 60
SLOT_DW = (1, 0, 2)
MESH = pl.DeviceIdType.MESH
F32, BF16 = jnp.float32, jnp.bfloat16


def dot(a, b):
    return jnp.dot(a, b, preferred_element_type=F32)


def dot_nt(a, b):
    return lax.dot_general(a, b, (((1,), (1,)), ((), ())), preferred_element_type=F32)


def kernel(
    n_tm, n_sc, reach,
    frames, conv_w, down_w, w_query, w_key, w_value, w_out, shots, labels, out_grad,
    latent_hbm, grad_hbm,
    latent_out, frame_grad, xin, gin, wb, wd, wqkv, wo, field, shift, taps, total, grouped, carry, mixes, kv, tokens, heads,
    edge_out, rim_out, edge_in, rim_in, tail_out, tail_in,
    w_sem, load_sem, store_sem, send_sem, recv_sem,
):
    T, R, W, C = xin.shape
    RC = R * C
    J = T // DOWN
    TW = T * W
    RIM = (KT - 1) * W
    M = TW + RIM
    NT = 256 if RC % 256 == 0 else C
    blocks = [slice(b, b + LANES) for b in range(0, RC, LANES)]
    i, s = lax.axis_index("tm"), lax.axis_index("scene")

    loads = []

    def load(src, dst):
        copy = pltpu.make_async_copy(src, dst, load_sem.at[len(loads)])
        copy.start()
        loads.append(copy)
        return copy

    get_x = load(frames, xin)
    w_copies = [[] for _ in SLOT_DW]
    count = 0
    for slot, dw in enumerate(SLOT_DW):
        for dt in range(KT):
            for ho in range(R):
                for hi in range(R):
                    copy = pltpu.make_async_copy(
                        conv_w.at[dt, hi - ho + 1, dw],
                        wb.at[dt, pl.ds(slot * RC + hi * C, C), pl.ds(ho * C, C)],
                        w_sem.at[count],
                    )
                    copy.start()
                    w_copies[slot].append(copy)
                    count += 1
    get_g = load(out_grad, gin)
    get_d = load(down_w, wd)
    get_qkv = [load(w, wqkv.at[:, pl.ds(k * C, C)]) for k, w in enumerate((w_query, w_key, w_value))]
    get_o = load(w_out, wo)

    barrier = pltpu.get_barrier_semaphore()
    peers = []
    for d in range(1, reach + 1):
        peers += [(i + d < n_tm, (i + d, s)), (i - d >= 0, (i - d, s))]
    for o in range(1, n_sc):
        peers.append((None, (i, lax.rem(s + o, n_sc))))
    for a in (-1, 1):
        for b in (-1, 1):
            ok = (i + a >= 0) & (i + a < n_tm) & (s + b >= 0) & (s + b < n_sc)
            peers.append((ok, (i + a, s + b)))
    waits = jnp.int32(0)
    for ok, dev in peers:
        if ok is None:
            pl.semaphore_signal(barrier, inc=1, device_id=dev, device_id_type=MESH)
            waits = waits + 1
        else:
            @pl.when(ok)
            def _(dev=dev):
                pl.semaphore_signal(barrier, inc=1, device_id=dev, device_id_type=MESH)

            waits = waits + ok.astype(jnp.int32)
    pending = []

    def send(ok, src, dst, k, dev):
        copy = pltpu.make_async_remote_copy(
            src_ref=src, dst_ref=dst, send_sem=send_sem.at[k], recv_sem=recv_sem.at[k],
            device_id=dev, device_id_type=MESH,
        )
        pl.when(ok)(copy.start)
        pending.append((ok, copy))

    def receive(ok, dst, k, zero=True):
        copy = pltpu.make_async_remote_copy(
            src_ref=dst, dst_ref=dst, send_sem=send_sem.at[k], recv_sem=recv_sem.at[k],
            device_id=(i, s), device_id_type=MESH,
        )
        pl.when(ok)(copy.wait_recv)
        if zero:
            @pl.when(jnp.logical_not(ok))
            def _():
                dst[...] = jnp.zeros(dst.shape, dst.dtype)

    left_ok, right_ok = s > 0, s < n_sc - 1

    def send_halo(phase):
        base = W + (RIM if phase == 0 else 0)
        step = 1 if phase == 0 else -1
        rim_ok = (i < n_tm - 1) if phase == 0 else (i > 0)
        rim_row = base + TW - RIM if phase == 0 else base
        for b, lanes in enumerate(blocks):
            edge_out[phase, 0, :, lanes] = field[b, pl.ds(base + W - 1, T, stride=W), :].astype(BF16)
            edge_out[phase, 1, :, lanes] = field[b, pl.ds(base, T, stride=W), :].astype(BF16)
            rim_out[phase, :, lanes] = field[b, pl.ds(rim_row, RIM), :].astype(BF16)
        if phase == 0:
            pl.semaphore_wait(barrier, waits)
        k = phase * 5
        rim = rim_out.at[phase]
        send(rim_ok, rim, rim_in.at[phase, 0], k, (i + step, s))
        send(right_ok, edge_out.at[phase, 0], edge_in.at[phase, 0], k + 3, (i, s + 1))
        send(left_ok, edge_out.at[phase, 1], edge_in.at[phase, 1], k + 4, (i, s - 1))
        send(rim_ok & right_ok, rim, rim_in.at[phase, 1], k + 1, (i + step, s + 1))
        send(rim_ok & left_ok, rim, rim_in.at[phase, 2], k + 2, (i + step, s - 1))

    def centre(phase):
        for b, lanes in enumerate(blocks):
            field[b, pl.ds(W if phase == 0 else W + TW, RIM), :] = jnp.zeros((RIM, LANES), F32)
            taps[:, lanes] = field[b, pl.ds(W, M), :].astype(BF16)

    def rim(phase):
        rim_ok = (i > 0) if phase == 0 else (i < n_tm - 1)
        receive(rim_ok, rim_in.at[phase, 0], phase * 5)
        for b, lanes in enumerate(blocks):
            field[b, pl.ds(W if phase == 0 else W + TW, RIM), :] = rim_in[phase, 0, :, lanes].astype(F32)
        own = rim_in[phase, 0]
        at = 0 if phase == 0 else TW - RIM

        @pl.loop(0, RC // NT)
        def _(n):
            cols = pl.ds(pl.multiple_of(n * NT, NT), NT)
            part = total[at : at + RIM, cols]
            for dt in range(KT - 1):
                if phase == 0:
                    y = dot(own, wb[dt, 0:RC, cols])
                    y = y[dt * W :]
                    low, high = 0, dt * W
                else:
                    y = dot_nt(own, wb[dt, cols, :])
                    y = y[: RIM - dt * W]
                    low, high = dt * W, 0
                pads = [jnp.zeros((low, NT), F32)] * (low > 0) + [y] + [jnp.zeros((high, NT), F32)] * (high > 0)
                part = part + (jnp.concatenate(pads, axis=0) if len(pads) > 1 else y)
            total[at : at + RIM, cols] = part

    def sides(phase, wanted=(0, 1)):
        rim_ok = (i > 0) if phase == 0 else (i < n_tm - 1)
        k = phase * 5
        inner = RIM if phase == 0 else 0
        outer = 0 if phase == 0 else TW
        for side in wanted:
            ok = left_ok if side == 0 else right_ok
            receive(ok, edge_in.at[phase, side], k + 3 + side)
            receive(ok & rim_ok, rim_in.at[phase, 1 + side], k + 1 + side)
            at = 0 if side == 0 else W - 1
            theirs = W - 1 if side == 0 else 0
            slot = 1 + side if phase == 0 else 2 - side
            for b, lanes in enumerate(blocks):
                shift[b] = field[b, pl.ds(W - 1 if side == 0 else W + 1, M), :]
                shift[b, pl.ds(inner + at, T, stride=W), :] = edge_in[phase, side, :, lanes].astype(F32)
                corner = rim_in[phase, 1 + side, :, lanes].astype(F32)
                for t in range(KT - 1):
                    row = t * W + theirs
                    shift[b, pl.ds(outer + t * W + at, 1), :] = corner[row : row + 1, :]
                taps[:, slot * RC + lanes.start : slot * RC + lanes.stop] = shift[b].astype(BF16)

    def conv(phase, first, slots, add):
        @pl.loop(0, RC // NT)
        def _(n):
            cols = pl.ds(pl.multiple_of(n * NT, NT), NT)
            part = total[:, cols] if add else None
            for dt in range(KT):
                if phase == 0:
                    lo = first * RC
                    y = dot(taps[:, lo : lo + slots * RC], wb[dt, pl.ds(lo, slots * RC), cols])
                    row = dt * W
                else:
                    row = (KT - 1 - dt) * W
                    y = None
                    for slot in range(first, first + slots):
                        rows = pl.ds(pl.multiple_of(slot * RC + n * NT, NT), NT)
                        z = dot_nt(taps[:, slot * RC : (slot + 1) * RC], wb[dt, rows, :])
                        y = z if y is None else y + z
                y = y[row : row + TW]
                part = y if part is None else part + y
            total[:, cols] = part

    get_x.wait()
    for b, lanes in enumerate(blocks):
        field[b, 0:W, :] = jnp.zeros((W, LANES), F32)
        field[b, W + M :, :] = jnp.zeros((W, LANES), F32)
        h = lanes.start // C
        own = xin[:, h, :, lanes.start - h * C : lanes.stop - h * C]
        field[b, W + RIM : W + M, :] = own.astype(F32).reshape(TW, LANES)
    send_halo(0)
    centre(0)
    for copy in w_copies[0]:
        copy.wait()
    conv(0, 0, 1, False)
    rim(0)
    sides(0)
    for copy in w_copies[1] + w_copies[2]:
        copy.wait()
    conv(0, 1, 2, True)

    get_g.wait()

    @pl.loop(0, J)
    def _(j):
        rows = pl.ds(pl.multiple_of(j * DOWN * W, DOWN * W), DOWN * W)
        span = pl.ds(pl.multiple_of(j * DOWN, DOWN), DOWN)
        for h in range(R):
            hc = slice(h * C, (h + 1) * C)
            pre = total[rows, hc]
            gate = jax.nn.sigmoid(pre)
            act = xin[span, h].astype(F32).reshape(DOWN * W, C) + pre * gate
            act = act.reshape(DOWN, W, C)
            for k in range(DOWN):
                grouped[pl.ds(pl.multiple_of((h * J + j) * W, W), W), k * C : (k + 1) * C] = act[k]
            slope = gate * (1.0 + pre * (1.0 - gate))
            grad = gin[span, h].astype(F32).reshape(DOWN * W, C) * slope
            for b, lanes in enumerate(blocks):
                if lanes.start // C == h:
                    own = grad[:, lanes.start - h * C : lanes.stop - h * C]
                    field[b, pl.ds(pl.multiple_of(W + j * DOWN * W, W), DOWN * W), :] = own

    send_halo(1)

    get_d.wait()
    kv[s] = dot(grouped[...].astype(BF16), wd[...].reshape(DOWN * C, C)).astype(BF16)
    starts, reached = [], jnp.int32(0)
    for k in range(shots.shape[0]):
        starts.append(reached)
        reached = reached + shots[k]

    def begin_of(t):
        best = jnp.int32(0)
        for start in starts:
            best = jnp.maximum(best, jnp.where(start <= t, start, 0))
        return best

    begins = [begin_of(i * J + j) for j in range(J)]

    def running_sums(latent):
        sums = [latent[:, 0]]
        for j in range(1, J):
            sums.append(latent[:, j] + sums[-1] * (begins[j] != i * J + j).astype(F32))
        return sums

    def latents(place):
        return kv[place].astype(F32).reshape(R, J, W, C)

    tail_out[...] = running_sums(latents(s))[-1]
    for d in range(1, reach + 1):
        send(i + d < n_tm, tail_out, tail_in.at[d - 1], 9 + d, (i + d, s))
    for o in range(1, n_sc):
        send(True, kv.at[s], kv.at[s], 9 + reach + o, (i, lax.rem(s + o, n_sc)))

    centre(1)
    conv(1, 0, 1, False)
    rim(1)
    sides(1, (1,))
    conv(1, 1, 1, True)

    carried = jnp.zeros((R, W, C), F32)
    open_from = begin_of(i * J - 1)
    for d in range(1, reach + 1):
        receive(i - d >= 0, tail_in.at[d - 1], 9 + d)
        carried = carried + tail_in[d - 1] * (open_from <= (i - d) * J + J - 1).astype(F32)
    carry[s] = carried
    for o in range(1, n_sc):
        send(True, carry.at[s], carry.at[s], 8 + reach + n_sc + o, (i, lax.rem(s + o, n_sc)))

    sides(1, (0,))
    conv(1, 2, 1, True)

    @pl.loop(0, J)
    def _(j):
        rows = pl.ds(pl.multiple_of(j * DOWN * W, DOWN * W), DOWN * W)
        span = pl.ds(pl.multiple_of(j * DOWN, DOWN), DOWN)
        for h in range(R):
            grad = gin[span, h].astype(F32) + total[rows, h * C : (h + 1) * C].reshape(DOWN, W, C)
            frame_grad[span, h] = grad.astype(BF16)

    put_grad = pltpu.make_async_copy(frame_grad, grad_hbm, store_sem.at[0])
    put_grad.start()

    for copy in get_qkv + [get_o]:
        copy.wait()
    Q = R * J * W
    K = n_sc * Q

    def mix(place):
        latent, before = latents(place), carry[place]
        sums = running_sums(latent)
        for j in range(J):
            shot_sum = sums[j] + before * (begins[j] < i * J).astype(F32)
            whole = latent[:, j] + shot_sum / (i * J + j - begins[j] + 1).astype(F32)
            mixes[:, j] = whole
        tokens[place] = mixes[...].reshape(Q, C).astype(BF16)

    mix(s)
    mixed = tokens[s]
    query = dot(mixed, wqkv[:, 0:C]).astype(BF16)

    def frame_of(shape, dim):
        place = lax.broadcasted_iota(jnp.int32, shape, dim)
        return lax.rem(lax.div(place, jnp.int32(W)), jnp.int32(J))

    frame_q, frame_k = frame_of((Q, 1), 0), frame_of((1, K), 1)
    label_q, label_k = jnp.zeros((Q, 1), jnp.int32), jnp.zeros((1, K), jnp.int32)
    for j in range(J):
        label_q = jnp.where(frame_q == j, labels[j], label_q)
        label_k = jnp.where(frame_k == j, labels[j], label_k)
    allowed = (label_q == label_k) & (frame_k <= frame_q)
    for o in range(1, n_sc):
        place = lax.rem(s + n_sc - o, n_sc)
        receive(s >= 0, kv.at[place], 9 + reach + o, False)
        receive(s >= 0, carry.at[place], 8 + reach + n_sc + o, False)
        mix(place)
    key_value = dot(tokens[...].reshape(K, C), wqkv[:, C:]).astype(BF16)
    per = 2
    lane = lax.broadcasted_iota(jnp.int32, (Q, per * HEAD), 1)
    for pair in range(C // (per * HEAD)):
        cols = slice(pair * per * HEAD, (pair + 1) * per * HEAD)
        q2, k2 = query[:, cols], key_value[:, cols]
        v2 = key_value[:, C + cols.start : C + cols.stop]
        out = None
        for one in range(per):
            mine = (lane >= one * HEAD) & (lane < (one + 1) * HEAD)
            q1 = jnp.where(mine, q2.astype(F32), 0.0).astype(BF16)
            scores = dot_nt(q1, k2) * (1.0 / math.sqrt(HEAD))
            scores = jnp.where(allowed, scores, -1000000000.0)
            expo = jnp.exp(scores - jnp.max(scores, axis=-1, keepdims=True))
            probs = (expo * (1.0 / jnp.sum(expo, axis=-1, keepdims=True))).astype(BF16)
            res = dot(probs, v2)
            out = res if out is None else jnp.where(mine, res, out)
        heads[:, cols] = out.astype(BF16)
    final = mixed.astype(F32) + dot(heads[...], wo[...])
    final = final.reshape(R, J, W, C)
    for h in range(R):
        latent_out[:, h] = final[h].astype(BF16)

    put_latent = pltpu.make_async_copy(latent_out, latent_hbm, store_sem.at[1])
    put_latent.start()
    put_grad.wait()
    put_latent.wait()
    for ok, copy in pending:
        pl.when(ok)(copy.wait_send)


def passing(steps, latent, grad, latent_to, grad_to, latent_at, grad_at, in_sem, out_sem):
    pieces = [(latent, latent_at, latent_to)]
    size = grad.shape[0] // steps
    for n in range(steps):
        rows = pl.ds(n * size, size)
        pieces.append((grad.at[rows], grad_at.at[rows], grad_to.at[rows]))
    takes = [pltpu.make_async_copy(a, b, in_sem.at[n]) for n, (a, b, _) in enumerate(pieces)]
    puts = [pltpu.make_async_copy(b, c, out_sem.at[n]) for n, (_, b, c) in enumerate(pieces)]
    for take in takes:
        take.start()
    for take, put in zip(takes, puts):
        take.wait()
        put.start()
    for put in puts:
        put.wait()


def hand_over(latent, grad):
    steps = math.gcd(4, grad.shape[0])
    spec = pl.BlockSpec(memory_space=pltpu.HBM)
    return pl.pallas_call(
        functools.partial(passing, steps),
        out_shape=tuple(jax.ShapeDtypeStruct(a.shape, a.dtype) for a in (latent, grad)),
        in_specs=[spec, spec],
        out_specs=(spec, spec),
        scratch_shapes=[
            pltpu.VMEM(latent.shape, latent.dtype),
            pltpu.VMEM(grad.shape, grad.dtype),
            pltpu.SemaphoreType.DMA((steps + 1,)),
            pltpu.SemaphoreType.DMA((steps + 1,)),
        ],
    )(latent, grad)


def per_device(n_tm, n_sc, frames, conv_w, down_w, w_query, w_key, w_value, w_out, shots, labels, out_grad):
    T, R, W, C = frames.shape
    J = T // DOWN
    RC = R * C
    TW = T * W
    RIM = (KT - 1) * W
    M = TW + RIM
    reach = max(1, n_tm // 2)
    any_spec = pl.BlockSpec(memory_space=pltpu.HBM)
    smem = pl.BlockSpec(memory_space=pltpu.SMEM)
    messages = 8 + reach + 2 * n_sc
    results = pl.pallas_call(
        functools.partial(kernel, n_tm, n_sc, reach),
        out_shape=(
            jax.ShapeDtypeStruct((J, R, W, C), BF16),
            jax.ShapeDtypeStruct((T, R, W, C), BF16),
        ),
        in_specs=[any_spec] * 7 + [smem, smem, any_spec],
        out_specs=(any_spec, any_spec),
        scratch_shapes=[
            pltpu.VMEM((J, R, W, C), BF16),
            pltpu.VMEM((T, R, W, C), BF16),
            pltpu.VMEM((T, R, W, C), BF16),
            pltpu.VMEM((T, R, W, C), BF16),
            pltpu.VMEM((KT, KW * RC, RC), BF16),
            pltpu.VMEM((DOWN, C, C), BF16),
            pltpu.VMEM((C, 3 * C), BF16),
            pltpu.VMEM((C, C), BF16),
            pltpu.VMEM((RC // LANES, M + 2 * W, LANES), F32),
            pltpu.VMEM((RC // LANES, M, LANES), F32),
            pltpu.VMEM((M, KW * RC), BF16),
            pltpu.VMEM((TW, RC), F32),
            pltpu.VMEM((R * J * W, DOWN * C), F32),
            pltpu.VMEM((n_sc, R, W, C), F32),
            pltpu.VMEM((R, J, W, C), F32),
            pltpu.VMEM((n_sc, R * J * W, C), BF16),
            pltpu.VMEM((n_sc, R * J * W, C), BF16),
            pltpu.VMEM((R * J * W, C), BF16),
            pltpu.VMEM((2, 2, T, RC), BF16),
            pltpu.VMEM((2, RIM, RC), BF16),
            pltpu.VMEM((2, 2, T, RC), BF16),
            pltpu.VMEM((2, 3, RIM, RC), BF16),
            pltpu.VMEM((R, W, C), F32),
            pltpu.VMEM((reach, R, W, C), F32),
            pltpu.SemaphoreType.DMA((KT * KW * R * R,)),
            pltpu.SemaphoreType.DMA((8,)),
            pltpu.SemaphoreType.DMA((2,)),
            pltpu.SemaphoreType.DMA((messages,)),
            pltpu.SemaphoreType.DMA((messages,)),
        ],
        compiler_params=pltpu.CompilerParams(
            collective_id=0, has_side_effects=True, vmem_limit_bytes=VMEM_MIB * 1024 * 1024
        ),
    )(frames, conv_w, down_w, w_query, w_key, w_value, w_out, shots, labels[:, 0], out_grad)
    return hand_over(*results)


def solution(mesh):
    in_specs = (
        P("tm", None, "scene", None), P(), P(), P(), P(), P(), P(), P(),
        P("tm", None), P("tm", None, "scene", None),
    )
    out_specs = (P("tm", None, "scene", None), P("tm", None, "scene", None))
    body = functools.partial(per_device, mesh.shape["tm"], mesh.shape["scene"])
    return jax.shard_map(body, mesh=mesh, in_specs=in_specs, out_specs=out_specs, check_vma=False)
```

profile of v0, /device:TPU:1, one launch (start us, length us, event | category | flops | bytes accessed | tf_op | source)
XLA Modules:
  0.0 34.1 jit_solution(12157758315724548843)
XLA Ops:
  0.6 31.5 %shard_map.113 = (bf16[8,2,8,384]{3,2,1,0:T(8,128)(2,1)}, bf16[64,2,8,384]{3,2,1,0:T(8,128)(2,1)}) custom-call(bf16[64,2,8,384]{3,2,1,0:T(8,128)(2,1)} %frames.1, bf16[3,3,3,384,384]{4,3,2,1,0:T(8,128)(2,1)} %conv_w.1, bf16[8,384,384]{2,1,0:T(8,128)(2,1)} %down_w.1, bf16[384,384]{1,0:T(8,128)(2,1)} %w_query.1, bf16[384,384]{1,0:T(8,128)(2,1)} %w_key.1, ...), custom_call_target="tpu_custom_call" | custom-call | tf_op jit(solution)/shard_map/pallas_call | solution.py:419
  32.1 2.0 %shard_map.114 = (bf16[8,2,8,384]{3,2,1,0:T(8,128)(2,1)}, bf16[64,2,8,384]{3,2,1,0:T(8,128)(2,1)}) custom-call(bf16[8,2,8,384]{3,2,1,0:T(8,128)(2,1)} %get-tuple-element.4.latent, bf16[64,2,8,384]{3,2,1,0:T(8,128)(2,1)} %get-tuple-element.5.grad), custom_call_target="tpu_custom_call" | custom-call | tf_op jit(solution)/shard_map/pallas_call | solution.py:394
where the time goes:
time: 34.3 us; the launch traced here: 34.1 us
  Pallas kernels  33.5 us (98%)
  between operations  0.64 us (2%)
    pallas_call x1, Pallas kernels, per_device(): pl.pallas_call(functools.partial(kernel, n_tm, n_sc, reach), out_shape=(j...  31.5 us
    pallas_call x1, Pallas kernels, hand_over(): pl.pallas_call(functools.partial(passing, steps), out_shape=tuple((jax.Sh...  2.03 us

commit v1 on v0

--- a/solution.py
+++ b/solution.py
@@ -12,7 +12,8 @@
 KT, KH, KW = 3, 3, 3
 DOWN = 8
 LANES = 128
-VMEM_MIB = 60
+VMEM_MIB = 63
+SPAN = 8
 SLOT_DW = (1, 0, 2)
 MESH = pl.DeviceIdType.MESH
 F32, BF16 = jnp.float32, jnp.bfloat16
@@ -28,11 +29,11 @@
 
 def kernel(
     n_tm, n_sc, reach,
-    frames, conv_w, down_w, w_query, w_key, w_value, w_out, shots, labels, out_grad,
-    latent_hbm, grad_hbm,
-    latent_out, frame_grad, xin, gin, wb, wd, wqkv, wo, field, shift, taps, total, grouped, carry, mixes, kv, tokens, heads,
-    edge_out, rim_out, edge_in, rim_in, tail_out, tail_in,
-    w_sem, load_sem, store_sem, send_sem, recv_sem,
+    frames, conv_w, down_w, w_query, w_key, w_value, w_out, shots_hbm, labels_hbm, out_grad,
+    latent_out, frame_grad,
+    shots, labels, xin, gin, wb, wd, wqkv, wo, field, shift, taps, total, grouped, carry, mixes, kv, tokens, heads,
+    edge_out, rim_out, edge_in, rim_in, corner_in, tail_out, tail_in,
+    w_sem, load_sem, send_sem, recv_sem,
 ):
     T, R, W, C = xin.shape
     RC = R * C
@@ -44,6 +45,7 @@
     blocks = [slice(b, b + LANES) for b in range(0, RC, LANES)]
     i, s = lax.axis_index("tm"), lax.axis_index("scene")
 
+    once = lax.div(i, jnp.int32(n_tm)) + 1
     loads = []
 
     def load(src, dst):
@@ -52,25 +54,23 @@
         loads.append(copy)
         return copy
 
-    get_x = load(frames, xin)
-    w_copies = [[] for _ in SLOT_DW]
-    count = 0
-    for slot, dw in enumerate(SLOT_DW):
-        for dt in range(KT):
-            for ho in range(R):
+    part = T // math.gcd(4, T)
+    get_x = [load(frames.at[pl.ds(t, part)], xin.at[pl.ds(t, part)]) for t in range(0, T, part)]
+    w_copies = [[[] for _ in range(R)] for _ in SLOT_DW]
+
+    def load_weights(slot):
+        for ho in range(R):
+            for dt in range(KT):
                 for hi in range(R):
                     copy = pltpu.make_async_copy(
-                        conv_w.at[dt, hi - ho + 1, dw],
+                        conv_w.at[dt, hi - ho + 1, SLOT_DW[slot]],
                         wb.at[dt, pl.ds(slot * RC + hi * C, C), pl.ds(ho * C, C)],
-                        w_sem.at[count],
+                        w_sem.at[((slot * R + ho) * KT + dt) * R + hi],
                     )
                     copy.start()
-                    w_copies[slot].append(copy)
-                    count += 1
-    get_g = load(out_grad, gin)
-    get_d = load(down_w, wd)
-    get_qkv = [load(w, wqkv.at[:, pl.ds(k * C, C)]) for k, w in enumerate((w_query, w_key, w_value))]
-    get_o = load(w_out, wo)
+                    w_copies[slot][ho].append(copy)
+
+    load_weights(0)
 
     barrier = pltpu.get_barrier_semaphore()
     peers = []
@@ -128,12 +128,13 @@
         if phase == 0:
             pl.semaphore_wait(barrier, waits)
         k = phase * 5
-        rim = rim_out.at[phase]
-        send(rim_ok, rim, rim_in.at[phase, 0], k, (i + step, s))
+        last = pl.ds(T - SPAN if phase == 0 else 0, SPAN)
+        right_edge, left_edge = edge_out.at[phase, 0, last], edge_out.at[phase, 1, last]
+        send(rim_ok & right_ok, right_edge, corner_in.at[phase, 0], k + 1, (i + step, s + 1))
+        send(rim_ok & left_ok, left_edge, corner_in.at[phase, 1], k + 2, (i + step, s - 1))
+        send(rim_ok, rim_out.at[phase], rim_in.at[phase], k, (i + step, s))
         send(right_ok, edge_out.at[phase, 0], edge_in.at[phase, 0], k + 3, (i, s + 1))
         send(left_ok, edge_out.at[phase, 1], edge_in.at[phase, 1], k + 4, (i, s - 1))
-        send(rim_ok & right_ok, rim, rim_in.at[phase, 1], k + 1, (i + step, s + 1))
-        send(rim_ok & left_ok, rim, rim_in.at[phase, 2], k + 2, (i + step, s - 1))
 
     def centre(phase):
         for b, lanes in enumerate(blocks):
@@ -142,10 +143,10 @@
 
     def rim(phase):
         rim_ok = (i > 0) if phase == 0 else (i < n_tm - 1)
-        receive(rim_ok, rim_in.at[phase, 0], phase * 5)
+        receive(rim_ok, rim_in.at[phase], phase * 5)
         for b, lanes in enumerate(blocks):
-            field[b, pl.ds(W if phase == 0 else W + TW, RIM), :] = rim_in[phase, 0, :, lanes].astype(F32)
-        own = rim_in[phase, 0]
+            field[b, pl.ds(W if phase == 0 else W + TW, RIM), :] = rim_in[phase, :, lanes].astype(F32)
+        own = rim_in[phase]
         at = 0 if phase == 0 else TW - RIM
 
         @pl.loop(0, RC // NT)
@@ -173,41 +174,54 @@
         for side in wanted:
             ok = left_ok if side == 0 else right_ok
             receive(ok, edge_in.at[phase, side], k + 3 + side)
-            receive(ok & rim_ok, rim_in.at[phase, 1 + side], k + 1 + side)
+            receive(ok & rim_ok, corner_in.at[phase, side], k + 1 + side)
             at = 0 if side == 0 else W - 1
-            theirs = W - 1 if side == 0 else 0
+            near = SPAN - (KT - 1) if phase == 0 else 0
             slot = 1 + side if phase == 0 else 2 - side
             for b, lanes in enumerate(blocks):
                 shift[b] = field[b, pl.ds(W - 1 if side == 0 else W + 1, M), :]
                 shift[b, pl.ds(inner + at, T, stride=W), :] = edge_in[phase, side, :, lanes].astype(F32)
-                corner = rim_in[phase, 1 + side, :, lanes].astype(F32)
+                corner = corner_in[phase, side, :, lanes].astype(F32)
                 for t in range(KT - 1):
-                    row = t * W + theirs
+                    row = near + t
                     shift[b, pl.ds(outer + t * W + at, 1), :] = corner[row : row + 1, :]
                 taps[:, slot * RC + lanes.start : slot * RC + lanes.stop] = shift[b].astype(BF16)
 
-    def conv(phase, first, slots, add):
-        @pl.loop(0, RC // NT)
-        def _(n):
-            cols = pl.ds(pl.multiple_of(n * NT, NT), NT)
+    def conv(phase, first, slots, add, tiles):
+        lo, hi = first * RC, (first + slots) * RC
+        def tile(n):
+            cols = slice(n * NT, (n + 1) * NT)
             part = total[:, cols] if add else None
             for dt in range(KT):
                 if phase == 0:
-                    lo = first * RC
-                    y = dot(taps[:, lo : lo + slots * RC], wb[dt, pl.ds(lo, slots * RC), cols])
                     row = dt * W
+                    ys = [dot(taps[row : row + TW, lo:hi], wb[dt, lo:hi, cols])]
                 else:
                     row = (KT - 1 - dt) * W
-                    y = None
-                    for slot in range(first, first + slots):
-                        rows = pl.ds(pl.multiple_of(slot * RC + n * NT, NT), NT)
-                        z = dot_nt(taps[:, slot * RC : (slot + 1) * RC], wb[dt, rows, :])
-                        y = z if y is None else y + z
-                y = y[row : row + TW]
-                part = y if part is None else part + y
+                    ys = []
+                    for at in range(lo, hi, RC):
+                        rows = slice(at + cols.start, at + cols.stop)
+                        ys.append(dot_nt(taps[row : row + TW, at : at + RC], wb[dt, rows, :]))
+                for y in ys:
+                    part = y if part is None else part + y
             total[:, cols] = part
 
-    get_x.wait()
+        @pl.loop(0, once)
+        def _(_):
+            for n in tiles:
+                tile(n)
+
+    every = range(RC // NT)
+
+    for copy in get_x:
+        copy.wait()
+    load_weights(1)
+    load_weights(2)
+    get_g = load(out_grad, gin)
+    get_d = load(down_w, wd)
+    get_qkv = [load(w, wqkv.at[:, pl.ds(k * C, C)]) for k, w in enumerate((w_query, w_key, w_value))]
+    get_o = load(w_out, wo)
+    get_index = [load(shots_hbm, shots), load(labels_hbm, labels)]
     for b, lanes in enumerate(blocks):
         field[b, 0:W, :] = jnp.zeros((W, LANES), F32)
         field[b, W + M :, :] = jnp.zeros((W, LANES), F32)
@@ -216,14 +230,19 @@
         field[b, W + RIM : W + M, :] = own.astype(F32).reshape(TW, LANES)
     send_halo(0)
     centre(0)
-    for copy in w_copies[0]:
-        copy.wait()
-    conv(0, 0, 1, False)
+    ready = 0
+    for n in every:
+        while ready * C < (n + 1) * NT:
+            for copy in w_copies[0][ready]:
+                copy.wait()
+            ready += 1
+        conv(0, 0, 1, False, (n,))
     rim(0)
     sides(0)
-    for copy in w_copies[1] + w_copies[2]:
-        copy.wait()
-    conv(0, 1, 2, True)
+    for copies in w_copies[1] + w_copies[2]:
+        for copy in copies:
+            copy.wait()
+    conv(0, 1, 2, True, every)
 
     get_g.wait()
 
@@ -249,7 +268,13 @@
     send_halo(1)
 
     get_d.wait()
-    kv[s] = dot(grouped[...].astype(BF16), wd[...].reshape(DOWN * C, C)).astype(BF16)
+
+    @pl.loop(0, once)
+    def _(_):
+        kv[s] = dot(grouped[...].astype(BF16), wd[...].reshape(DOWN * C, C)).astype(BF16)
+
+    for copy in get_index:
+        copy.wait()
     starts, reached = [], jnp.int32(0)
     for k in range(shots.shape[0]):
         starts.append(reached)
@@ -275,14 +300,33 @@
     tail_out[...] = running_sums(latents(s))[-1]
     for d in range(1, reach + 1):
         send(i + d < n_tm, tail_out, tail_in.at[d - 1], 9 + d, (i + d, s))
-    for o in range(1, n_sc):
-        send(True, kv.at[s], kv.at[s], 9 + reach + o, (i, lax.rem(s + o, n_sc)))
+    sibling = s + 1 - 2 * lax.rem(s, 2)
+    far = range(1, n_sc // 2)
+    hops = 1 + 2 * len(far)
+
+    def spread(ref, k):
+        send(True, ref.at[s], ref.at[s], k, (i, sibling))
+        for o in far:
+            send(True, ref.at[s], ref.at[s], k + o, (i, lax.rem(s + 2 * o, n_sc)))
+
+    def relay(ref, k):
+        for o in far:
+            place = lax.rem(s + n_sc - 2 * o, n_sc)
+            receive(s >= 0, ref.at[place], k + o, False)
+            send(True, ref.at[place], ref.at[place], k + len(far) + o, (i, sibling))
+
+    def arrive(ref, k):
+        receive(s >= 0, ref.at[sibling], k, False)
+        for o in far:
+            place = lax.rem(sibling + n_sc - 2 * o, n_sc)
+            receive(s >= 0, ref.at[place], k + len(far) + o, False)
+
+    k_kv = 10 + reach
+    k_carry = k_kv + hops
+    spread(kv, k_kv)
 
     centre(1)
-    conv(1, 0, 1, False)
-    rim(1)
-    sides(1, (1,))
-    conv(1, 1, 1, True)
+    conv(1, 0, 1, False, every)
 
     carried = jnp.zeros((R, W, C), F32)
     open_from = begin_of(i * J - 1)
@@ -290,11 +334,14 @@
         receive(i - d >= 0, tail_in.at[d - 1], 9 + d)
         carried = carried + tail_in[d - 1] * (open_from <= (i - d) * J + J - 1).astype(F32)
     carry[s] = carried
-    for o in range(1, n_sc):
-        send(True, carry.at[s], carry.at[s], 8 + reach + n_sc + o, (i, lax.rem(s + o, n_sc)))
-
-    sides(1, (0,))
-    conv(1, 2, 1, True)
+    spread(carry, k_carry)
+
+    rim(1)
+    sides(1)
+    conv(1, 1, 2, True, every[:1])
+    relay(kv, k_kv)
+    relay(carry, k_carry)
+    conv(1, 1, 2, True, every[1:])
 
     @pl.loop(0, J)
     def _(j):
@@ -303,9 +350,6 @@
         for h in range(R):
             grad = gin[span, h].astype(F32) + total[rows, h * C : (h + 1) * C].reshape(DOWN, W, C)
             frame_grad[span, h] = grad.astype(BF16)
-
-    put_grad = pltpu.make_async_copy(frame_grad, grad_hbm, store_sem.at[0])
-    put_grad.start()
 
     for copy in get_qkv + [get_o]:
         copy.wait()
@@ -335,11 +379,10 @@
         label_q = jnp.where(frame_q == j, labels[j], label_q)
         label_k = jnp.where(frame_k == j, labels[j], label_k)
     allowed = (label_q == label_k) & (frame_k <= frame_q)
+    arrive(kv, k_kv)
+    arrive(carry, k_carry)
     for o in range(1, n_sc):
-        place = lax.rem(s + n_sc - o, n_sc)
-        receive(s >= 0, kv.at[place], 9 + reach + o, False)
-        receive(s >= 0, carry.at[place], 8 + reach + n_sc + o, False)
-        mix(place)
+        mix(lax.rem(s + n_sc - o, n_sc))
     key_value = dot(tokens[...].reshape(K, C), wqkv[:, C:]).astype(BF16)
     per = 2
     lane = lax.broadcasted_iota(jnp.int32, (Q, per * HEAD), 1)
@@ -363,45 +406,26 @@
     for h in range(R):
         latent_out[:, h] = final[h].astype(BF16)
 
-    put_latent = pltpu.make_async_copy(latent_out, latent_hbm, store_sem.at[1])
-    put_latent.start()
-    put_grad.wait()
-    put_latent.wait()
     for ok, copy in pending:
         pl.when(ok)(copy.wait_send)
 
 
-def passing(steps, latent, grad, latent_to, grad_to, latent_at, grad_at, in_sem, out_sem):
-    pieces = [(latent, latent_at, latent_to)]
-    size = grad.shape[0] // steps
-    for n in range(steps):
-        rows = pl.ds(n * size, size)
-        pieces.append((grad.at[rows], grad_at.at[rows], grad_to.at[rows]))
-    takes = [pltpu.make_async_copy(a, b, in_sem.at[n]) for n, (a, b, _) in enumerate(pieces)]
-    puts = [pltpu.make_async_copy(b, c, out_sem.at[n]) for n, (_, b, c) in enumerate(pieces)]
-    for take in takes:
-        take.start()
-    for take, put in zip(takes, puts):
-        take.wait()
+def passing(latent, grad, latent_to, grad_to, sem):
+    puts = [pltpu.make_async_copy(grad, grad_to, sem.at[0]), pltpu.make_async_copy(latent, latent_to, sem.at[1])]
+    for put in puts:
         put.start()
     for put in puts:
         put.wait()
 
 
 def hand_over(latent, grad):
-    steps = math.gcd(4, grad.shape[0])
-    spec = pl.BlockSpec(memory_space=pltpu.HBM)
+    latent, grad = (pltpu.with_memory_space_constraint(a, pltpu.VMEM) for a in (latent, grad))
     return pl.pallas_call(
-        functools.partial(passing, steps),
+        passing,
         out_shape=tuple(jax.ShapeDtypeStruct(a.shape, a.dtype) for a in (latent, grad)),
-        in_specs=[spec, spec],
-        out_specs=(spec, spec),
-        scratch_shapes=[
-            pltpu.VMEM(latent.shape, latent.dtype),
-            pltpu.VMEM(grad.shape, grad.dtype),
-            pltpu.SemaphoreType.DMA((steps + 1,)),
-            pltpu.SemaphoreType.DMA((steps + 1,)),
-        ],
+        in_specs=[pl.BlockSpec(memory_space=pltpu.VMEM)] * 2,
+        out_specs=(pl.BlockSpec(memory_space=pltpu.HBM),) * 2,
+        scratch_shapes=[pltpu.SemaphoreType.DMA((2,))],
     )(latent, grad)
 
 
@@ -414,19 +438,19 @@
     M = TW + RIM
     reach = max(1, n_tm // 2)
     any_spec = pl.BlockSpec(memory_space=pltpu.HBM)
-    smem = pl.BlockSpec(memory_space=pltpu.SMEM)
-    messages = 8 + reach + 2 * n_sc
+    vmem = pl.BlockSpec(memory_space=pltpu.VMEM)
+    messages = 10 + reach + 2 * (n_sc - 1)
     results = pl.pallas_call(
         functools.partial(kernel, n_tm, n_sc, reach),
         out_shape=(
-            jax.ShapeDtypeStruct((J, R, W, C), BF16),
-            jax.ShapeDtypeStruct((T, R, W, C), BF16),
-        ),
-        in_specs=[any_spec] * 7 + [smem, smem, any_spec],
-        out_specs=(any_spec, any_spec),
-        scratch_shapes=[
             pltpu.VMEM((J, R, W, C), BF16),
             pltpu.VMEM((T, R, W, C), BF16),
+        ),
+        in_specs=[any_spec] * 10,
+        out_specs=(vmem, vmem),
+        scratch_shapes=[
+            pltpu.SMEM(shots.shape, jnp.int32),
+            pltpu.SMEM((J,), jnp.int32),
             pltpu.VMEM((T, R, W, C), BF16),
             pltpu.VMEM((T, R, W, C), BF16),
             pltpu.VMEM((KT, KW * RC, RC), BF16),
@@ -446,12 +470,12 @@
             pltpu.VMEM((2, 2, T, RC), BF16),
             pltpu.VMEM((2, RIM, RC), BF16),
             pltpu.VMEM((2, 2, T, RC), BF16),
-            pltpu.VMEM((2, 3, RIM, RC), BF16),
+            pltpu.VMEM((2, RIM, RC), BF16),
+            pltpu.VMEM((2, 2, SPAN, RC), BF16),
             pltpu.VMEM((R, W, C), F32),
             pltpu.VMEM((reach, R, W, C), F32),
             pltpu.SemaphoreType.DMA((KT * KW * R * R,)),
-            pltpu.SemaphoreType.DMA((8,)),
-            pltpu.SemaphoreType.DMA((2,)),
+            pltpu.SemaphoreType.DMA((13,)),
             pltpu.SemaphoreType.DMA((messages,)),
             pltpu.SemaphoreType.DMA((messages,)),
         ],

time: 34.3 us -> 28.8 us (0.84)
  the two profiles are of different devices: /device:TPU:1 before, /device:TPU:25 now
where the time goes in v1:
time: 28.8 us; the launch traced here: 28.6 us
  Pallas kernels  28 us (97%)
  between operations  0.64 us (2%)
    pallas_call x1, Pallas kernels, per_device(): pl.pallas_call(functools.partial(kernel, n_tm, n_sc, reach), out_shape=(p...  27.1 us
    pallas_call x1, Pallas kernels, hand_over(): pl.pallas_call(passing, out_shape=tuple((jax.ShapeDtypeStruct(a.shape, a....  0.92 us

profile of v1, /device:TPU:25, one launch (start us, length us, event | category | flops | bytes accessed | tf_op | source)
XLA Modules:
  0.0 28.6 jit_solution(16091143604672861355)
XLA Ops:
  0.6 27.1 %shard_map.113 = (bf16[8,2,8,384]{3,2,1,0:T(8,128)(2,1)S(1)}, bf16[64,2,8,384]{3,2,1,0:T(8,128)(2,1)S(1)}) custom-call(bf16[64,2,8,384]{3,2,1,0:T(8,128)(2,1)} %frames.1, bf16[3,3,3,384,384]{4,3,2,1,0:T(8,128)(2,1)} %conv_w.1, bf16[8,384,384]{2,1,0:T(8,128)(2,1)} %down_w.1, bf16[384,384]{1,0:T(8,128)(2,1)} %w_query.1, bf16[384,384]{1,0:T(8,128)(2,1)} %w_key.1, ...), custom_call_target="tpu_custom_call" | custom-call | tf_op jit(solution)/shard_map/pallas_call | solution.py:443
  27.7 0.9 %shard_map.114 = (bf16[8,2,8,384]{3,2,1,0:T(8,128)(2,1)}, bf16[64,2,8,384]{3,2,1,0:T(8,128)(2,1)}) custom-call(bf16[8,2,8,384]{3,2,1,0:T(8,128)(2,1)S(1)} %get-tuple-element.4.latent, bf16[64,2,8,384]{3,2,1,0:T(8,128)(2,1)S(1)} %get-tuple-element.5.grad), custom_call_target="tpu_custom_call" | custom-call | tf_op jit(solution)/shard_map/pallas_call | solution.py:423

commit v2 on v1

--- a/solution.py
+++ b/solution.py
@@ -328,19 +328,20 @@
     centre(1)
     conv(1, 0, 1, False, every)
 
+    rim(1)
+    sides(1)
+    conv(1, 1, 2, True, every[:1])
+    relay(kv, k_kv)
+
     carried = jnp.zeros((R, W, C), F32)
     open_from = begin_of(i * J - 1)
     for d in range(1, reach + 1):
         receive(i - d >= 0, tail_in.at[d - 1], 9 + d)
         carried = carried + tail_in[d - 1] * (open_from <= (i - d) * J + J - 1).astype(F32)
     carry[s] = carried
-    spread(carry, k_carry)
-
-    rim(1)
-    sides(1)
-    conv(1, 1, 2, True, every[:1])
-    relay(kv, k_kv)
-    relay(carry, k_carry)
+    for o in range(1, n_sc):
+        send(True, carry.at[s], carry.at[s], k_carry - 1 + o, (i, lax.rem(s + o, n_sc)))
+
     conv(1, 1, 2, True, every[1:])
 
     @pl.loop(0, J)
@@ -380,26 +381,26 @@
         label_k = jnp.where(frame_k == j, labels[j], label_k)
     allowed = (label_q == label_k) & (frame_k <= frame_q)
     arrive(kv, k_kv)
-    arrive(carry, k_carry)
     for o in range(1, n_sc):
-        mix(lax.rem(s + n_sc - o, n_sc))
+        place = lax.rem(s + n_sc - o, n_sc)
+        receive(s >= 0, carry.at[place], k_carry - 1 + o, False)
+        mix(place)
     key_value = dot(tokens[...].reshape(K, C), wqkv[:, C:]).astype(BF16)
     per = 2
     lane = lax.broadcasted_iota(jnp.int32, (Q, per * HEAD), 1)
     for pair in range(C // (per * HEAD)):
         cols = slice(pair * per * HEAD, (pair + 1) * per * HEAD)
-        q2, k2 = query[:, cols], key_value[:, cols]
+        q2, k2 = query[:, cols].astype(F32) * (1.0 / math.sqrt(HEAD)), key_value[:, cols]
         v2 = key_value[:, C + cols.start : C + cols.stop]
-        out = None
-        for one in range(per):
-            mine = (lane >= one * HEAD) & (lane < (one + 1) * HEAD)
-            q1 = jnp.where(mine, q2.astype(F32), 0.0).astype(BF16)
-            scores = dot_nt(q1, k2) * (1.0 / math.sqrt(HEAD))
-            scores = jnp.where(allowed, scores, -1000000000.0)
-            expo = jnp.exp(scores - jnp.max(scores, axis=-1, keepdims=True))
-            probs = (expo * (1.0 / jnp.sum(expo, axis=-1, keepdims=True))).astype(BF16)
-            res = dot(probs, v2)
-            out = res if out is None else jnp.where(mine, res, out)
+        mine = [(lane >= one * HEAD) & (lane < (one + 1) * HEAD) for one in range(per)]
+        q1 = jnp.concatenate([jnp.where(m, q2, 0.0) for m in mine], axis=0).astype(BF16)
+        scores = jnp.where(allowed[None], dot_nt(q1, k2).reshape(per, Q, K), -1000000000.0)
+        expo = jnp.exp(scores - jnp.max(scores, axis=-1, keepdims=True))
+        scale = 1.0 / jnp.sum(expo, axis=-1, keepdims=True)
+        res = dot(expo.astype(BF16).reshape(per * Q, K), v2).reshape(per, Q, per * HEAD) * scale
+        out = res[0]
+        for one in range(1, per):
+            out = jnp.where(mine[one], res[one], out)
         heads[:, cols] = out.astype(BF16)
     final = mixed.astype(F32) + dot(heads[...], wo[...])
     final = final.reshape(R, J, W, C)

time: 28.8 us -> 26.6 us (0.924)
  the two profiles are of different devices: /device:TPU:25 before, /device:TPU:0 now
where the time goes in v2:
time: 26.6 us; the launch traced here: 26.4 us
  Pallas kernels  25.8 us (97%)
  between operations  0.64 us (2%)
    pallas_call x1, Pallas kernels, per_device(): pl.pallas_call(functools.partial(kernel, n_tm, n_sc, reach), out_shape=(p...  24.9 us
    pallas_call x1, Pallas kernels, hand_over(): pl.pallas_call(passing, out_shape=tuple((jax.ShapeDtypeStruct(a.shape, a....  0.92 us

profile of v2, /device:TPU:0, one launch (start us, length us, event | category | flops | bytes accessed | tf_op | source)
XLA Modules:
  0.0 26.4 jit_solution(3106503970933118043)
XLA Ops:
  0.6 24.9 %shard_map.113 = (bf16[8,2,8,384]{3,2,1,0:T(8,128)(2,1)S(1)}, bf16[64,2,8,384]{3,2,1,0:T(8,128)(2,1)S(1)}) custom-call(bf16[64,2,8,384]{3,2,1,0:T(8,128)(2,1)} %frames.1, bf16[3,3,3,384,384]{4,3,2,1,0:T(8,128)(2,1)} %conv_w.1, bf16[8,384,384]{2,1,0:T(8,128)(2,1)} %down_w.1, bf16[384,384]{1,0:T(8,128)(2,1)} %w_query.1, bf16[384,384]{1,0:T(8,128)(2,1)} %w_key.1, ...), custom_call_target="tpu_custom_call" | custom-call | tf_op jit(solution)/shard_map/pallas_call | solution.py:444
  25.5 0.9 %shard_map.114 = (bf16[8,2,8,384]{3,2,1,0:T(8,128)(2,1)}, bf16[64,2,8,384]{3,2,1,0:T(8,128)(2,1)}) custom-call(bf16[8,2,8,384]{3,2,1,0:T(8,128)(2,1)S(1)} %get-tuple-element.4.latent, bf16[64,2,8,384]{3,2,1,0:T(8,128)(2,1)S(1)} %get-tuple-element.5.grad), custom_call_target="tpu_custom_call" | custom-call | tf_op jit(solution)/shard_map/pallas_call | solution.py:424

commit v3 on v2

--- a/solution.py
+++ b/solution.py
@@ -130,9 +130,9 @@
         k = phase * 5
         last = pl.ds(T - SPAN if phase == 0 else 0, SPAN)
         right_edge, left_edge = edge_out.at[phase, 0, last], edge_out.at[phase, 1, last]
+        send(rim_ok, rim_out.at[phase], rim_in.at[phase], k, (i + step, s))
         send(rim_ok & right_ok, right_edge, corner_in.at[phase, 0], k + 1, (i + step, s + 1))
         send(rim_ok & left_ok, left_edge, corner_in.at[phase, 1], k + 2, (i + step, s - 1))
-        send(rim_ok, rim_out.at[phase], rim_in.at[phase], k, (i + step, s))
         send(right_ok, edge_out.at[phase, 0], edge_in.at[phase, 0], k + 3, (i, s + 1))
         send(left_ok, edge_out.at[phase, 1], edge_in.at[phase, 1], k + 4, (i, s - 1))
 
@@ -146,25 +146,14 @@
         receive(rim_ok, rim_in.at[phase], phase * 5)
         for b, lanes in enumerate(blocks):
             field[b, pl.ds(W if phase == 0 else W + TW, RIM), :] = rim_in[phase, :, lanes].astype(F32)
-        own = rim_in[phase]
-        at = 0 if phase == 0 else TW - RIM
-
-        @pl.loop(0, RC // NT)
-        def _(n):
-            cols = pl.ds(pl.multiple_of(n * NT, NT), NT)
-            part = total[at : at + RIM, cols]
-            for dt in range(KT - 1):
-                if phase == 0:
-                    y = dot(own, wb[dt, 0:RC, cols])
-                    y = y[dt * W :]
-                    low, high = 0, dt * W
-                else:
-                    y = dot_nt(own, wb[dt, cols, :])
-                    y = y[: RIM - dt * W]
-                    low, high = dt * W, 0
-                pads = [jnp.zeros((low, NT), F32)] * (low > 0) + [y] + [jnp.zeros((high, NT), F32)] * (high > 0)
-                part = part + (jnp.concatenate(pads, axis=0) if len(pads) > 1 else y)
-            total[at : at + RIM, cols] = part
+
+    def shift_rows(phase, side, row, rows):
+        for b in range(len(blocks)):
+            shift[side, b, pl.ds(row, rows), :] = field[b, pl.ds((W - 1 if side == 0 else W + 1) + row, rows), :]
+
+    def shift_own(phase):
+        for side in (0, 1):
+            shift_rows(phase, side, RIM if phase == 0 else 0, TW)
 
     def sides(phase, wanted=(0, 1)):
         rim_ok = (i > 0) if phase == 0 else (i < n_tm - 1)
@@ -178,14 +167,14 @@
             at = 0 if side == 0 else W - 1
             near = SPAN - (KT - 1) if phase == 0 else 0
             slot = 1 + side if phase == 0 else 2 - side
+            shift_rows(phase, side, outer, RIM)
             for b, lanes in enumerate(blocks):
-                shift[b] = field[b, pl.ds(W - 1 if side == 0 else W + 1, M), :]
-                shift[b, pl.ds(inner + at, T, stride=W), :] = edge_in[phase, side, :, lanes].astype(F32)
+                shift[side, b, pl.ds(inner + at, T, stride=W), :] = edge_in[phase, side, :, lanes].astype(F32)
                 corner = corner_in[phase, side, :, lanes].astype(F32)
                 for t in range(KT - 1):
                     row = near + t
-                    shift[b, pl.ds(outer + t * W + at, 1), :] = corner[row : row + 1, :]
-                taps[:, slot * RC + lanes.start : slot * RC + lanes.stop] = shift[b].astype(BF16)
+                    shift[side, b, pl.ds(outer + t * W + at, 1), :] = corner[row : row + 1, :]
+                taps[:, slot * RC + lanes.start : slot * RC + lanes.stop] = shift[side, b].astype(BF16)
 
     def conv(phase, first, slots, add, tiles):
         lo, hi = first * RC, (first + slots) * RC
@@ -205,9 +194,22 @@
                 for y in ys:
                     part = y if part is None else part + y
             total[:, cols] = part
+            if not add:
+                return
+            own = rim_in[phase]
+            for dt in range(KT - 1):
+                if phase == 0:
+                    y = dot(own, wb[dt, 0:RC, cols])[dt * W :]
+                    at = 0
+                else:
+                    y = dot_nt(own, wb[dt, cols, :])[: RIM - dt * W]
+                    at = TW - RIM + dt * W
+                total[at : at + RIM - dt * W, cols] = total[at : at + RIM - dt * W, cols] + y
 
         @pl.loop(0, once)
         def _(_):
+            if not add and tiles[0] == 0:
+                shift_own(phase)
             for n in tiles:
                 tile(n)
 
@@ -217,11 +219,6 @@
         copy.wait()
     load_weights(1)
     load_weights(2)
-    get_g = load(out_grad, gin)
-    get_d = load(down_w, wd)
-    get_qkv = [load(w, wqkv.at[:, pl.ds(k * C, C)]) for k, w in enumerate((w_query, w_key, w_value))]
-    get_o = load(w_out, wo)
-    get_index = [load(shots_hbm, shots), load(labels_hbm, labels)]
     for b, lanes in enumerate(blocks):
         field[b, 0:W, :] = jnp.zeros((W, LANES), F32)
         field[b, W + M :, :] = jnp.zeros((W, LANES), F32)
@@ -237,6 +234,11 @@
                 copy.wait()
             ready += 1
         conv(0, 0, 1, False, (n,))
+    get_g = load(out_grad, gin)
+    get_d = load(down_w, wd)
+    get_qkv = [load(w, wqkv.at[:, pl.ds(k * C, C)]) for k, w in enumerate((w_query, w_key, w_value))]
+    get_o = load(w_out, wo)
+    get_index = [load(shots_hbm, shots), load(labels_hbm, labels)]
     rim(0)
     sides(0)
     for copies in w_copies[1] + w_copies[2]:
@@ -304,11 +306,6 @@
     far = range(1, n_sc // 2)
     hops = 1 + 2 * len(far)
 
-    def spread(ref, k):
-        send(True, ref.at[s], ref.at[s], k, (i, sibling))
-        for o in far:
-            send(True, ref.at[s], ref.at[s], k + o, (i, lax.rem(s + 2 * o, n_sc)))
-
     def relay(ref, k):
         for o in far:
             place = lax.rem(s + n_sc - 2 * o, n_sc)
@@ -323,16 +320,16 @@
 
     k_kv = 10 + reach
     k_carry = k_kv + hops
-    spread(kv, k_kv)
+    send(True, kv.at[s], kv.at[s], k_kv, (i, sibling))
 
     centre(1)
     conv(1, 0, 1, False, every)
+    for o in far:
+        send(True, kv.at[s], kv.at[s], k_kv + o, (i, lax.rem(s + 2 * o, n_sc)))
 
     rim(1)
     sides(1)
     conv(1, 1, 2, True, every[:1])
-    relay(kv, k_kv)
-
     carried = jnp.zeros((R, W, C), F32)
     open_from = begin_of(i * J - 1)
     for d in range(1, reach + 1):
@@ -342,7 +339,9 @@
     for o in range(1, n_sc):
         send(True, carry.at[s], carry.at[s], k_carry - 1 + o, (i, lax.rem(s + o, n_sc)))
 
-    conv(1, 1, 2, True, every[1:])
+    conv(1, 1, 2, True, every[1:2])
+    relay(kv, k_kv)
+    conv(1, 1, 2, True, every[2:])
 
     @pl.loop(0, J)
     def _(j):
@@ -459,7 +458,7 @@
             pltpu.VMEM((C, 3 * C), BF16),
             pltpu.VMEM((C, C), BF16),
             pltpu.VMEM((RC // LANES, M + 2 * W, LANES), F32),
-            pltpu.VMEM((RC // LANES, M, LANES), F32),
+            pltpu.VMEM((2, RC // LANES, M, LANES), F32),
             pltpu.VMEM((M, KW * RC), BF16),
             pltpu.VMEM((TW, RC), F32),
             pltpu.VMEM((R * J * W, DOWN * C), F32),

time: 26.6 us -> 25.7 us (0.966)
  the two profiles are of different devices: /device:TPU:0 before, /device:TPU:1 now
where the time goes in v3:
time: 25.7 us; the launch traced here: 25.5 us
  Pallas kernels  24.9 us (97%)
  between operations  0.64 us (2%)
    pallas_call x1, Pallas kernels, per_device(): pl.pallas_call(functools.partial(kernel, n_tm, n_sc, reach), out_shape=(p...  24 us
    pallas_call x1, Pallas kernels, hand_over(): pl.pallas_call(passing, out_shape=tuple((jax.ShapeDtypeStruct(a.shape, a....  0.92 us

profile of v3, /device:TPU:1, one launch (start us, length us, event | category | flops | bytes accessed | tf_op | source)
XLA Modules:
  0.0 25.5 jit_solution(8835286960765471831)
XLA Ops:
  0.6 24.0 %shard_map.113 = (bf16[8,2,8,384]{3,2,1,0:T(8,128)(2,1)S(1)}, bf16[64,2,8,384]{3,2,1,0:T(8,128)(2,1)S(1)}) custom-call(bf16[64,2,8,384]{3,2,1,0:T(8,128)(2,1)} %frames.1, bf16[3,3,3,384,384]{4,3,2,1,0:T(8,128)(2,1)} %conv_w.1, bf16[8,384,384]{2,1,0:T(8,128)(2,1)} %down_w.1, bf16[384,384]{1,0:T(8,128)(2,1)} %w_query.1, bf16[384,384]{1,0:T(8,128)(2,1)} %w_key.1, ...), custom_call_target="tpu_custom_call" | custom-call | tf_op jit(solution)/shard_map/pallas_call | solution.py:443
  24.6 0.9 %shard_map.114 = (bf16[8,2,8,384]{3,2,1,0:T(8,128)(2,1)}, bf16[64,2,8,384]{3,2,1,0:T(8,128)(2,1)}) custom-call(bf16[8,2,8,384]{3,2,1,0:T(8,128)(2,1)S(1)} %get-tuple-element.4.latent, bf16[64,2,8,384]{3,2,1,0:T(8,128)(2,1)S(1)} %get-tuple-element.5.grad), custom_call_target="tpu_custom_call" | custom-call | tf_op jit(solution)/shard_map/pallas_call | solution.py:423

commit v4 on v3

--- a/solution.py
+++ b/solution.py
@@ -136,9 +136,9 @@
         send(right_ok, edge_out.at[phase, 0], edge_in.at[phase, 0], k + 3, (i, s + 1))
         send(left_ok, edge_out.at[phase, 1], edge_in.at[phase, 1], k + 4, (i, s - 1))
 
-    def centre(phase):
+    def centre():
         for b, lanes in enumerate(blocks):
-            field[b, pl.ds(W if phase == 0 else W + TW, RIM), :] = jnp.zeros((RIM, LANES), F32)
+            field[b, W : W + RIM, :] = jnp.zeros((RIM, LANES), F32)
             taps[:, lanes] = field[b, pl.ds(W, M), :].astype(BF16)
 
     def rim(phase):
@@ -205,6 +205,14 @@
                     y = dot_nt(own, wb[dt, cols, :])[: RIM - dt * W]
                     at = TW - RIM + dt * W
                 total[at : at + RIM - dt * W, cols] = total[at : at + RIM - dt * W, cols] + y
+            if phase == 0:
+                return
+            for lanes in blocks:
+                if cols.start <= lanes.start < cols.stop:
+                    h = lanes.start // C
+                    spot = slice(lanes.start - h * C, lanes.stop - h * C)
+                    grad = gin[:, h, :, spot].astype(F32) + total[:, lanes].reshape(T, W, LANES)
+                    frame_grad[:, h, :, spot] = grad.astype(BF16)
 
         @pl.loop(0, once)
         def _(_):
@@ -226,7 +234,7 @@
         own = xin[:, h, :, lanes.start - h * C : lanes.stop - h * C]
         field[b, W + RIM : W + M, :] = own.astype(F32).reshape(TW, LANES)
     send_halo(0)
-    centre(0)
+    centre()
     ready = 0
     for n in every:
         while ready * C < (n + 1) * NT:
@@ -266,6 +274,7 @@
                 if lanes.start // C == h:
                     own = grad[:, lanes.start - h * C : lanes.stop - h * C]
                     field[b, pl.ds(pl.multiple_of(W + j * DOWN * W, W), DOWN * W), :] = own
+                    taps[rows, lanes] = own.astype(BF16)
 
     send_halo(1)
 
@@ -322,7 +331,7 @@
     k_carry = k_kv + hops
     send(True, kv.at[s], kv.at[s], k_kv, (i, sibling))
 
-    centre(1)
+    taps[TW:, 0:RC] = jnp.zeros((RIM, RC), BF16)
     conv(1, 0, 1, False, every)
     for o in far:
         send(True, kv.at[s], kv.at[s], k_kv + o, (i, lax.rem(s + 2 * o, n_sc)))
@@ -343,14 +352,6 @@
     relay(kv, k_kv)
     conv(1, 1, 2, True, every[2:])
 
-    @pl.loop(0, J)
-    def _(j):
-        rows = pl.ds(pl.multiple_of(j * DOWN * W, DOWN * W), DOWN * W)
-        span = pl.ds(pl.multiple_of(j * DOWN, DOWN), DOWN)
-        for h in range(R):
-            grad = gin[span, h].astype(F32) + total[rows, h * C : (h + 1) * C].reshape(DOWN, W, C)
-            frame_grad[span, h] = grad.astype(BF16)
-
     for copy in get_qkv + [get_o]:
         copy.wait()
     Q = R * J * W
@@ -366,45 +367,48 @@
         tokens[place] = mixes[...].reshape(Q, C).astype(BF16)
 
     mix(s)
-    mixed = tokens[s]
-    query = dot(mixed, wqkv[:, 0:C]).astype(BF16)
-
-    def frame_of(shape, dim):
-        place = lax.broadcasted_iota(jnp.int32, shape, dim)
-        return lax.rem(lax.div(place, jnp.int32(W)), jnp.int32(J))
-
-    frame_q, frame_k = frame_of((Q, 1), 0), frame_of((1, K), 1)
-    label_q, label_k = jnp.zeros((Q, 1), jnp.int32), jnp.zeros((1, K), jnp.int32)
-    for j in range(J):
-        label_q = jnp.where(frame_q == j, labels[j], label_q)
-        label_k = jnp.where(frame_k == j, labels[j], label_k)
-    allowed = (label_q == label_k) & (frame_k <= frame_q)
     arrive(kv, k_kv)
     for o in range(1, n_sc):
         place = lax.rem(s + n_sc - o, n_sc)
         receive(s >= 0, carry.at[place], k_carry - 1 + o, False)
         mix(place)
-    key_value = dot(tokens[...].reshape(K, C), wqkv[:, C:]).astype(BF16)
-    per = 2
-    lane = lax.broadcasted_iota(jnp.int32, (Q, per * HEAD), 1)
-    for pair in range(C // (per * HEAD)):
-        cols = slice(pair * per * HEAD, (pair + 1) * per * HEAD)
-        q2, k2 = query[:, cols].astype(F32) * (1.0 / math.sqrt(HEAD)), key_value[:, cols]
-        v2 = key_value[:, C + cols.start : C + cols.stop]
-        mine = [(lane >= one * HEAD) & (lane < (one + 1) * HEAD) for one in range(per)]
-        q1 = jnp.concatenate([jnp.where(m, q2, 0.0) for m in mine], axis=0).astype(BF16)
-        scores = jnp.where(allowed[None], dot_nt(q1, k2).reshape(per, Q, K), -1000000000.0)
-        expo = jnp.exp(scores - jnp.max(scores, axis=-1, keepdims=True))
-        scale = 1.0 / jnp.sum(expo, axis=-1, keepdims=True)
-        res = dot(expo.astype(BF16).reshape(per * Q, K), v2).reshape(per, Q, per * HEAD) * scale
-        out = res[0]
-        for one in range(1, per):
-            out = jnp.where(mine[one], res[one], out)
-        heads[:, cols] = out.astype(BF16)
-    final = mixed.astype(F32) + dot(heads[...], wo[...])
-    final = final.reshape(R, J, W, C)
-    for h in range(R):
-        latent_out[:, h] = final[h].astype(BF16)
+
+    @pl.loop(0, once)
+    def _(_):
+        mixed = tokens[s]
+        query = dot(mixed, wqkv[:, 0:C]).astype(BF16)
+
+        def frame_of(shape, dim):
+            place = lax.broadcasted_iota(jnp.int32, shape, dim)
+            return lax.rem(lax.div(place, jnp.int32(W)), jnp.int32(J))
+
+        frame_q, frame_k = frame_of((Q, 1), 0), frame_of((1, K), 1)
+        label_q, label_k = jnp.zeros((Q, 1), jnp.int32), jnp.zeros((1, K), jnp.int32)
+        for j in range(J):
+            label_q = jnp.where(frame_q == j, labels[j], label_q)
+            label_k = jnp.where(frame_k == j, labels[j], label_k)
+        allowed = (label_q == label_k) & (frame_k <= frame_q)
+        key_value = dot(tokens[...].reshape(K, C), wqkv[:, C:]).astype(BF16)
+        per = 2
+        lane = lax.broadcasted_iota(jnp.int32, (Q, per * HEAD), 1)
+        for pair in range(C // (per * HEAD)):
+            cols = slice(pair * per * HEAD, (pair + 1) * per * HEAD)
+            q2, k2 = query[:, cols].astype(F32) * (1.0 / math.sqrt(HEAD)), key_value[:, cols]
+            v2 = key_value[:, C + cols.start : C + cols.stop]
+            mine = [(lane >= one * HEAD) & (lane < (one + 1) * HEAD) for one in range(per)]
+            q1 = jnp.concatenate([jnp.where(m, q2, 0.0) for m in mine], axis=0).astype(BF16)
+            scores = jnp.where(allowed[None], dot_nt(q1, k2).reshape(per, Q, K), -1000000000.0)
+            expo = jnp.exp(scores - jnp.max(scores, axis=-1, keepdims=True))
+            scale = 1.0 / jnp.sum(expo, axis=-1, keepdims=True)
+            res = dot(expo.astype(BF16).reshape(per * Q, K), v2).reshape(per, Q, per * HEAD) * scale
+            out = res[0]
+            for one in range(1, per):
+                out = jnp.where(mine[one], res[one], out)
+            heads[:, cols] = out.astype(BF16)
+        final = mixed.astype(F32) + dot(heads[...], wo[...])
+        final = final.reshape(R, J, W, C)
+        for h in range(R):
+            latent_out[:, h] = final[h].astype(BF16)
 
     for ok, copy in pending:
         pl.when(ok)(copy.wait_send)

time: 25.7 us -> 25.4 us (0.988)
  Pallas kernels: 24.9 us -> 24.6 us
    pallas_call x1, Pallas kernels: 24 us -> 23.7 us  [per_device(): pl.pallas_call(functools.partial(kernel, n_tm, n_sc, reach), out_shape=(p...]
where the time goes in v4:
time: 25.4 us; the launch traced here: 25.2 us
  Pallas kernels  24.6 us (97%)
  between operations  0.64 us (3%)
    pallas_call x1, Pallas kernels, per_device(): pl.pallas_call(functools.partial(kernel, n_tm, n_sc, reach), out_shape=(p...  23.7 us
    pallas_call x1, Pallas kernels, hand_over(): pl.pallas_call(passing, out_shape=tuple((jax.ShapeDtypeStruct(a.shape, a....  0.92 us

profile of v4, /device:TPU:1, one launch (start us, length us, event | category | flops | bytes accessed | tf_op | source)
XLA Modules:
  0.0 25.2 jit_solution(17560460800157727514)
XLA Ops:
  0.6 23.7 %shard_map.113 = (bf16[8,2,8,384]{3,2,1,0:T(8,128)(2,1)S(1)}, bf16[64,2,8,384]{3,2,1,0:T(8,128)(2,1)S(1)}) custom-call(bf16[64,2,8,384]{3,2,1,0:T(8,128)(2,1)} %frames.1, bf16[3,3,3,384,384]{4,3,2,1,0:T(8,128)(2,1)} %conv_w.1, bf16[8,384,384]{2,1,0:T(8,128)(2,1)} %down_w.1, bf16[384,384]{1,0:T(8,128)(2,1)} %w_query.1, bf16[384,384]{1,0:T(8,128)(2,1)} %w_key.1, ...), custom_call_target="tpu_custom_call" | custom-call | tf_op jit(solution)/shard_map/pallas_call | solution.py:447
  24.3 0.9 %shard_map.114 = (bf16[8,2,8,384]{3,2,1,0:T(8,128)(2,1)}, bf16[64,2,8,384]{3,2,1,0:T(8,128)(2,1)}) custom-call(bf16[8,2,8,384]{3,2,1,0:T(8,128)(2,1)S(1)} %get-tuple-element.4.latent, bf16[64,2,8,384]{3,2,1,0:T(8,128)(2,1)S(1)} %get-tuple-element.5.grad), custom_call_target="tpu_custom_call" | custom-call | tf_op jit(solution)/shard_map/pallas_call | solution.py:427
